TPU v7x, 512 devices: a whole 4x4x16 slice. The times are simulated.
512 devices in a mesh: plane: 16 (over x, z_hi), tile: 32 (over z_lo, y, core).
Axes of the slice: x: 4, y: 4, z: 16 (z_hi: 4, z_lo: 4; z = z_hi * 4 + z_lo), core: 2. Of those that a mesh axis runs over, the one named last changes fastest.
Arguments:
- density: float32 [48, 256, 2048], P('plane', 'tile'), may hold values from -6 to 6
- plane_slot: int32 [48], replicated, may hold values from 0 to 95, as said below
- paint_weight: float32 [32, 9], replicated, may hold values from -2 to 2
- paint_bias: float32 [32], replicated, may hold values from -0.5 to 0.5
- mix_weight: float32 [32], replicated, may hold values from -1 to 1
- short_kernel: float32 [5, 5], replicated, may hold values from -1 to 1
Outputs:
- distortion: float32 [4, 48, 256, 2048], P(None, 'plane', 'tile')
Inputs may be any that keep to these rules, and one draw needn't show every extreme that they name: `plane_slot`: strictly increasing along the planes; the first is 0 and the last is 95.
All inputs are finite; a program needn't handle non-finite values.
Results may differ from a plain program's by a relative error of at most 0.00026.
Values sent between devices are 32-bit elements; how exact they have to be, the bound alone decides.
No kernel may reach another device: no remote copies, remote signals or barrier semaphores. Data moves between devices by JAX's collectives and lax.ppermute only.
A program may use at most 64 MiB of HBM per device.

v0:
```python
import math
import jax
import jax.numpy as jnp
from jax import lax
from jax.sharding import PartitionSpec as P

highest = lax.Precision.HIGHEST
lens_gain = 0.25


def extended_2(block, sides, width):
    for axis, dim in sides:
        count = lax.axis_size(axis)
        forward = [(i, i + 1) for i in range(count - 1)]
        backward = [(target, source) for source, target in forward]
        low = lax.ppermute(
            lax.slice_in_dim(block, block.shape[dim] - width, None, axis=dim), axis, forward
        )
        high = lax.ppermute(lax.slice_in_dim(block, 0, width, axis=dim), axis, backward)
        block = jnp.concatenate([low, block, high], axis=dim)
    return block


def from_behind(value, axis, by):
    devices = lax.axis_size(axis)
    pairs = [(i, i + by) for i in range(devices) if 0 <= i + by < devices]
    return lax.ppermute(value, axis, pairs)


def paint_rows(extended, paint_weight, paint_bias, mix_weight):
    row_count = extended.shape[-2] - 4
    col_count = extended.shape[-1]
    padded = jnp.pad(extended, [(0, 0)] * (extended.ndim - 1) + [(2, 2)])
    stacked = jnp.stack(
        [
            padded[
                ...,
                2 + 2 * row_step : 2 + 2 * row_step + row_count,
                2 + 2 * col_step : 2 + 2 * col_step + col_count,
            ]
            for row_step in (-1, 0, 1)
            for col_step in (-1, 0, 1)
        ],
        axis=0,
    )
    before = jnp.einsum("ct,t...->c...", paint_weight, stacked, precision=highest)
    hidden = jnp.tanh(before + paint_bias.reshape((-1,) + (1,) * (before.ndim - 1)))
    return jnp.einsum("c,c...->...", mix_weight, hidden, precision=highest)


def short_rows(extended, short_kernel):
    row_count = extended.shape[-2] - 4
    col_count = extended.shape[-1]
    padded = jnp.pad(extended, [(0, 0)] * (extended.ndim - 1) + [(2, 2)])
    running = jnp.zeros(extended.shape[:-2] + (row_count, col_count), jnp.float32)
    for row_tap in range(5):
        for col_tap in range(5):
            running = (
                running
                + short_kernel[row_tap, col_tap]
                * padded[..., row_tap : row_tap + row_count, col_tap : col_tap + col_count]
            )
    return running


def hessian_rows(extended):
    padded = jnp.pad(extended, [(0, 0)] * (extended.ndim - 1) + [(1, 1)])
    center = padded[..., 1:-1, 1:-1]
    second_rows = padded[..., 2:, 1:-1] - 2.0 * center + padded[..., :-2, 1:-1]
    second_cols = padded[..., 1:-1, 2:] - 2.0 * center + padded[..., 1:-1, :-2]
    mixed_part = (
        padded[..., 2:, 2:] - padded[..., 2:, :-2] - padded[..., :-2, 2:] + padded[..., :-2, :-2]
    ) * 0.25
    return jnp.stack([second_rows, second_cols, mixed_part], axis=0)


def lens_step(lens_state, shear_field, mixing, bending):
    previous = lens_state[0:2]
    current = lens_state[2:4]
    bent_first = shear_field[0] * current[0] + shear_field[2] * current[1]
    bent_second = shear_field[2] * current[0] + shear_field[1] * current[1]
    bent_rows = jnp.stack([bent_first, bent_second], axis=0)
    advanced = (1.0 - mixing) * previous + mixing * current - bending * bent_rows
    return jnp.concatenate([current, advanced], axis=0)


def distances(plane_slot, slot_total):
    distance = (plane_slot.astype(jnp.float32) + 1.0) / slot_total
    before = jnp.concatenate([jnp.zeros((1,), jnp.float32), distance[:-1]])
    after = jnp.concatenate(
        [distance[1:], jnp.full((1,), (slot_total + 1.0) / slot_total, jnp.float32)]
    )
    mixing = before * (after - distance) / (distance * (after - before))
    bending = lens_gain * (after - distance) / after
    return (mixing, bending)


def coarse_kernel(row_global, col_global, scale):
    gap = row_global.astype(jnp.float32)[:, None] - col_global.astype(jnp.float32)[None, :]
    return jnp.exp(-jnp.abs(gap) / scale)


def start_for(row_count, col_count):
    pattern = jnp.array([[1.0, 0.0], [0.0, 1.0], [1.0, 0.0], [0.0, 1.0]], jnp.float32)
    return jnp.broadcast_to(pattern[:, :, None, None], (4, 2, row_count, col_count))


def body(density, plane_slot, paint_weight, paint_bias, mix_weight, short_kernel):
    plane_count, row_count, col_count = density.shape
    tile_count = lax.axis_size("tile")
    tile_index = lax.axis_index("tile")
    plane_index = lax.axis_index("plane")
    total_rows = row_count * tile_count
    coarse_here = row_count // 4
    coarse_cols = col_count // 4
    row_scale = total_rows / 16.0
    col_scale = col_count / 16.0
    long_gain = 1.0 / math.sqrt(row_scale * col_scale)
    col_kernel = coarse_kernel(
        jnp.arange(coarse_cols, dtype=jnp.int32),
        jnp.arange(coarse_cols, dtype=jnp.int32),
        col_scale,
    )
    mixing_all, bending_all = distances(plane_slot, 2 * plane_slot.shape[0])
    mixing_here = lax.dynamic_slice_in_dim(mixing_all, plane_index * plane_count, plane_count)
    bending_here = lax.dynamic_slice_in_dim(bending_all, plane_index * plane_count, plane_count)
    extended = extended_2(density, (("tile", 1),), 2)
    convergence = paint_rows(extended, paint_weight, paint_bias, mix_weight)
    convergence_wide = extended_2(convergence, (("tile", 1),), 2)
    short_part = short_rows(convergence_wide, short_kernel)
    row_global = tile_index * coarse_here + 0 + jnp.arange(coarse_here, dtype=jnp.int32)
    coarse = convergence.reshape(plane_count, coarse_here, 4, coarse_cols, 4).mean(axis=(2, 4))
    received = lax.all_gather(coarse, "tile", axis=1, tiled=True)
    span_cols = received.shape[1]
    kernel_block = coarse_kernel(row_global, jnp.arange(span_cols, dtype=jnp.int32), row_scale)
    summed = jnp.einsum("ik,pkx->pix", kernel_block, received, precision=highest)
    potential = short_part + jnp.repeat(
        jnp.repeat(
            long_gain * jnp.einsum("pix,xy->piy", summed, col_kernel, precision=highest), 4, axis=1
        ),
        4,
        axis=2,
    )
    potential_wide = extended_2(potential, (("tile", 1),), 1)
    shear_field = hessian_rows(potential_wide)

    def run_planes(lens_state):
        results = []
        for plane_pos in range(plane_count):
            lens_state = lens_step(
                lens_state,
                shear_field[:, plane_pos],
                mixing_here[plane_pos],
                bending_here[plane_pos],
            )
            results.append(lens_state[2:4].reshape(4, row_count, col_count))
        return (lens_state, jnp.stack(results, axis=1))

    start_state = start_for(row_count, col_count)

    def relay_turn(iteration, state_in):
        state_out, unused_results = run_planes(state_in)
        incoming = from_behind(state_out, "plane", 1)
        return jnp.where(plane_index == 0, start_state, incoming)

    state_in = lax.fori_loop(0, lax.axis_size("plane") - 1, relay_turn, start_state)
    unused_state, results = run_planes(state_in)
    return results


def solution(mesh):
    placed = (P("plane", "tile", None), P(), P(), P(), P(), P())
    return jax.shard_map(
        body, mesh=mesh, in_specs=placed, out_specs=P(None, "plane", "tile", None), check_vma=False
    )
```

profile of v0, /device:TPU:108, one launch (start us, length us, event | category | flops | bytes accessed | tf_op | source)
XLA Modules:
  0.0 1031.1 jit_solution(7631755121506922006)
XLA Ops:
  24.1 6.6 stack.90
  30.8 7.6 fusion.61
  43.0 7.9 reshape.65
  59.8 36.7 %all_gather.3 = f32[3,64,512]{2,0,1:T(4,128)S(1)} all-gather(f32[3,2,512]{2,0,1:T(4,128)S(1)} %copy.220), channel_id=1, replica_groups=mesh['plane'=16,'tile'=32] {'tile'}, dimensions={1}, use_global_device_ids=true | all-gather | bytes 405504 | tf_op jit(solution)/shard_map/all_gather | solution.py:133
  102.8 17.4 %fusion.33 = f32[3,8,2048]{2,1,0:T(8,128)S(1)} fusion(f32[3,8,2048]{2,1,0:T(8,128)S(1)} %copy.225, f32[3,8,2048]{2,1,0:T(8,128)S(1)} %bitcast.137, f32[3,2,2048]{2,1,0:T(2,128)} %collective-permute-done.4, f32[3,2,2048]{2,1,0:T(2,128)} %collective-permute-done.3, f32[3,12,2052]{2,1,0:T(8,128)S(1)} %select_maximum_fusion.2, f32[]{:T(128)} %bitcast.37, ...), kind=kLoop, calls=%fused_computation.74 | loop fusion | flops 2654208 | bytes 4620388 | tf_op jit(solution)/shard_map/add | solution.py:137
  128.2 895.2 %while.13 = (s32[]{:T(128)}, f32[4,2,8,2048]{3,2,1,0:T(8,128)S(1)}, pred[]{:T(512)}, f32[]{:T(128)}, f32[3]{0:T(128)S(1)}, /*index=5*/f32[]{:T(128)}, f32[3]{0:T...) while((s32[]{:T(128)}, f32[4,2,8,2048]{3,2,1,0:T(8,128)S(1)}, ...), condition=%wide.region_2.3_spmd.clone, body=%wide.region_1.2_spmd.sunk.clone.sunk | while | flops 2818050 | bytes 11469090 | solution.py:166
  135.6 9.1 collective-permute-start
  144.7 35.9 %collective-permute-done = f32[4,2,8,2048]{3,2,1,0:T(8,128)S(1)} collective-permute-done((f32[4,2,8,2048]{3,2,1,0:T(8,128)S(1)}, f32[4,2,8,2048]{3,2,1,0:T(8,128)S(1)}, u32[]{:S(2)}, u32[]{:S(2)}) %collective-permute-start) | collective-permute-done | bytes 524320 | tf_op jit(solution)/shard_map/while/body/eval_jaxpr/ppermute | solution.py:27
  188.2 6.8 collective-permute-start
  195.0 27.6 %collective-permute-done = f32[4,2,8,2048]{3,2,1,0:T(8,128)S(1)} collective-permute-done((f32[4,2,8,2048]{3,2,1,0:T(8,128)S(1)}, f32[4,2,8,2048]{3,2,1,0:T(8,128)S(1)}, u32[]{:S(2)}, u32[]{:S(2)}) %collective-permute-start) | collective-permute-done | bytes 524320 | tf_op jit(solution)/shard_map/while/body/eval_jaxpr/ppermute | solution.py:27
  232.1 90.6 %collective-permute-done = f32[4,2,8,2048]{3,2,1,0:T(8,128)S(1)} collective-permute-done((f32[4,2,8,2048]{3,2,1,0:T(8,128)S(1)}, f32[4,2,8,2048]{3,2,1,0:T(8,128)S(1)}, u32[]{:S(2)}, u32[]{:S(2)}) %collective-permute-start) | collective-permute-done | bytes 524320 | tf_op jit(solution)/shard_map/while/body/eval_jaxpr/ppermute | solution.py:27
  330.2 8.4 collective-permute-start
  338.6 54.5 %collective-permute-done = f32[4,2,8,2048]{3,2,1,0:T(8,128)S(1)} collective-permute-done((f32[4,2,8,2048]{3,2,1,0:T(8,128)S(1)}, f32[4,2,8,2048]{3,2,1,0:T(8,128)S(1)}, u32[]{:S(2)}, u32[]{:S(2)}) %collective-permute-start) | collective-permute-done | bytes 524320 | tf_op jit(solution)/shard_map/while/body/eval_jaxpr/ppermute | solution.py:27
  402.6 14.2 %collective-permute-done = f32[4,2,8,2048]{3,2,1,0:T(8,128)S(1)} collective-permute-done((f32[4,2,8,2048]{3,2,1,0:T(8,128)S(1)}, f32[4,2,8,2048]{3,2,1,0:T(8,128)S(1)}, u32[]{:S(2)}, u32[]{:S(2)}) %collective-permute-start) | collective-permute-done | bytes 524320 | tf_op jit(solution)/shard_map/while/body/eval_jaxpr/ppermute | solution.py:27
  424.4 78.4 %collective-permute-start = (f32[4,2,8,2048]{3,2,1,0:T(8,128)S(1)}, f32[4,2,8,2048]{3,2,1,0:T(8,128)S(1)}, u32[]{:S(2)}, u32[]{:S(2)}) collective-permute-start(f32[4,2,8,2048]{3,2,1,0:T(8,128)S(1)} %pad_maximum_fusion.12), channel_id=1, source_target_pairs={{0,32},{32,64},{64,96},{96,128},{128,160},{160,192},{192,224},{224... | collective-permute-start | bytes 1572872 | tf_op jit(solution)/shard_map/while/body/eval_jaxpr/ppermute | solution.py:27
  502.8 10.5 %collective-permute-done = f32[4,2,8,2048]{3,2,1,0:T(8,128)S(1)} collective-permute-done((f32[4,2,8,2048]{3,2,1,0:T(8,128)S(1)}, f32[4,2,8,2048]{3,2,1,0:T(8,128)S(1)}, u32[]{:S(2)}, u32[]{:S(2)}) %collective-permute-start) | collective-permute-done | bytes 524320 | tf_op jit(solution)/shard_map/while/body/eval_jaxpr/ppermute | solution.py:27
  520.9 38.9 %collective-permute-start = (f32[4,2,8,2048]{3,2,1,0:T(8,128)S(1)}, f32[4,2,8,2048]{3,2,1,0:T(8,128)S(1)}, u32[]{:S(2)}, u32[]{:S(2)}) collective-permute-start(f32[4,2,8,2048]{3,2,1,0:T(8,128)S(1)} %pad_maximum_fusion.12), channel_id=1, source_target_pairs={{0,32},{32,64},{64,96},{96,128},{128,160},{160,192},{192,224},{224... | collective-permute-start | bytes 1572872 | tf_op jit(solution)/shard_map/while/body/eval_jaxpr/ppermute | solution.py:27
  559.8 9.2 collective-permute-done
  576.6 86.0 %collective-permute-start = (f32[4,2,8,2048]{3,2,1,0:T(8,128)S(1)}, f32[4,2,8,2048]{3,2,1,0:T(8,128)S(1)}, u32[]{:S(2)}, u32[]{:S(2)}) collective-permute-start(f32[4,2,8,2048]{3,2,1,0:T(8,128)S(1)} %pad_maximum_fusion.12), channel_id=1, source_target_pairs={{0,32},{32,64},{64,96},{96,128},{128,160},{160,192},{192,224},{224... | collective-permute-start | bytes 1572872 | tf_op jit(solution)/shard_map/while/body/eval_jaxpr/ppermute | solution.py:27
  662.6 70.1 %collective-permute-done = f32[4,2,8,2048]{3,2,1,0:T(8,128)S(1)} collective-permute-done((f32[4,2,8,2048]{3,2,1,0:T(8,128)S(1)}, f32[4,2,8,2048]{3,2,1,0:T(8,128)S(1)}, u32[]{:S(2)}, u32[]{:S(2)}) %collective-permute-start) | collective-permute-done | bytes 524320 | tf_op jit(solution)/shard_map/while/body/eval_jaxpr/ppermute | solution.py:27
  740.3 38.8 %collective-permute-start = (f32[4,2,8,2048]{3,2,1,0:T(8,128)S(1)}, f32[4,2,8,2048]{3,2,1,0:T(8,128)S(1)}, u32[]{:S(2)}, u32[]{:S(2)}) collective-permute-start(f32[4,2,8,2048]{3,2,1,0:T(8,128)S(1)} %pad_maximum_fusion.12), channel_id=1, source_target_pairs={{0,32},{32,64},{64,96},{96,128},{128,160},{160,192},{192,224},{224... | collective-permute-start | bytes 1572872 | tf_op jit(solution)/shard_map/while/body/eval_jaxpr/ppermute | solution.py:27
  779.2 52.8 %collective-permute-done = f32[4,2,8,2048]{3,2,1,0:T(8,128)S(1)} collective-permute-done((f32[4,2,8,2048]{3,2,1,0:T(8,128)S(1)}, f32[4,2,8,2048]{3,2,1,0:T(8,128)S(1)}, u32[]{:S(2)}, u32[]{:S(2)}) %collective-permute-start) | collective-permute-done | bytes 524320 | tf_op jit(solution)/shard_map/while/body/eval_jaxpr/ppermute | solution.py:27
  839.5 8.3 collective-permute-start
  847.8 27.7 %collective-permute-done = f32[4,2,8,2048]{3,2,1,0:T(8,128)S(1)} collective-permute-done((f32[4,2,8,2048]{3,2,1,0:T(8,128)S(1)}, f32[4,2,8,2048]{3,2,1,0:T(8,128)S(1)}, u32[]{:S(2)}, u32[]{:S(2)}) %collective-permute-start) | collective-permute-done | bytes 524320 | tf_op jit(solution)/shard_map/while/body/eval_jaxpr/ppermute | solution.py:27
  883.2 8.3 collective-permute-start
  891.5 7.7 collective-permute-done
  906.8 12.1 %collective-permute-start = (f32[4,2,8,2048]{3,2,1,0:T(8,128)S(1)}, f32[4,2,8,2048]{3,2,1,0:T(8,128)S(1)}, u32[]{:S(2)}, u32[]{:S(2)}) collective-permute-start(f32[4,2,8,2048]{3,2,1,0:T(8,128)S(1)} %pad_maximum_fusion.12), channel_id=1, source_target_pairs={{0,32},{32,64},{64,96},{96,128},{128,160},{160,192},{192,224},{224... | collective-permute-start | bytes 1572872 | tf_op jit(solution)/shard_map/while/body/eval_jaxpr/ppermute | solution.py:27
  918.9 12.8 %collective-permute-done = f32[4,2,8,2048]{3,2,1,0:T(8,128)S(1)} collective-permute-done((f32[4,2,8,2048]{3,2,1,0:T(8,128)S(1)}, f32[4,2,8,2048]{3,2,1,0:T(8,128)S(1)}, u32[]{:S(2)}, u32[]{:S(2)}) %collective-permute-start) | collective-permute-done | bytes 524320 | tf_op jit(solution)/shard_map/while/body/eval_jaxpr/ppermute | solution.py:27
  939.2 8.3 collective-permute-start
  947.5 20.1 %collective-permute-done = f32[4,2,8,2048]{3,2,1,0:T(8,128)S(1)} collective-permute-done((f32[4,2,8,2048]{3,2,1,0:T(8,128)S(1)}, f32[4,2,8,2048]{3,2,1,0:T(8,128)S(1)}, u32[]{:S(2)}, u32[]{:S(2)}) %collective-permute-start) | collective-permute-done | bytes 524320 | tf_op jit(solution)/shard_map/while/body/eval_jaxpr/ppermute | solution.py:27
  978.2 21.6 %collective-permute-done = f32[4,2,8,2048]{3,2,1,0:T(8,128)S(1)} collective-permute-done((f32[4,2,8,2048]{3,2,1,0:T(8,128)S(1)}, f32[4,2,8,2048]{3,2,1,0:T(8,128)S(1)}, u32[]{:S(2)}, u32[]{:S(2)}) %collective-permute-start) | collective-permute-done | bytes 524320 | tf_op jit(solution)/shard_map/while/body/eval_jaxpr/ppermute | solution.py:27
  1009.3 14.0 %collective-permute-done = f32[4,2,8,2048]{3,2,1,0:T(8,128)S(1)} collective-permute-done((f32[4,2,8,2048]{3,2,1,0:T(8,128)S(1)}, f32[4,2,8,2048]{3,2,1,0:T(8,128)S(1)}, u32[]{:S(2)}, u32[]{:S(2)}) %collective-permute-start) | collective-permute-done | bytes 524320 | tf_op jit(solution)/shard_map/while/body/eval_jaxpr/ppermute | solution.py:27
  (234 shorter events, 179.1 us)
Async XLA Ops:
  0.0 30.7 %copy-start = (f32[32,9]{0,1:T(8,128)S(1)}, f32[32,9]{0,1:T(8,128)}, u32[]{:S(2)}) copy-start(f32[32,9]{0,1:T(8,128)} %param.11) | copy-start | bytes 3460
  1.1 14.3 %collective-permute-start.1 = (f32[3,2,2048]{2,1,0:T(2,128)S(1)}, f32[3,2,2048]{2,1,0:T(2,128)S(1)}, u32[]{:S(2)}, u32[]{:S(2)}) collective-permute-start(f32[3,2,2048]{2,1,0:T(2,128)S(1)} %get-tuple-element.225), channel_id=1, source_target_pairs={{0,1},{1,2},{2,3},{3,4},{4,5},{5,6},{6,7},{7,8},{8,9},{9,10},{10,1... | collective-permute-start | bytes 147464 | tf_op jit(solution)/shard_map/ppermute | solution.py:16
  3.0 12.4 %collective-permute-start.2 = (f32[3,2,2048]{2,1,0:T(2,128)S(1)}, f32[3,2,2048]{2,1,0:T(2,128)S(1)}, u32[]{:S(2)}, u32[]{:S(2)}) collective-permute-start(f32[3,2,2048]{2,1,0:T(2,128)S(1)} %get-tuple-element.226), channel_id=1, source_target_pairs={{1,0},{2,1},{3,2},{4,3},{5,4},{6,5},{7,6},{8,7},{9,8},{10,9},{11,1... | collective-permute-start | bytes 147464 | tf_op jit(solution)/shard_map/ppermute | solution.py:19
  30.7 7.6 copy-start.5
  30.8 7.6 copy-start.6
  43.0 53.4 %copy-start.3 = (f32[64]{0:T(128)S(1)}, f32[64]{0:T(128)}, u32[]{:S(2)}) copy-start(f32[64]{0:T(128)} %iota_convert_fusion.1) | copy-start | bytes 772
  43.0 53.4 %copy-start.4 = (f32[2]{0:T(128)S(1)}, f32[2]{0:T(128)}, u32[]{:S(2)}) copy-start(f32[2]{0:T(128)} %add_convert_fusion) | copy-start | bytes 28
  43.0 53.9 %copy-start.2 = (f32[512]{0:T(512)S(1)}, f32[512]{0:T(512)}, u32[]{:S(2)}) copy-start(f32[512]{0:T(512)} %iota_convert_fusion) | copy-start | bytes 6148
  50.9 50.8 %collective-permute-start.3 = (f32[3,2,2048]{2,1,0:T(2,128)}, f32[3,2,2048]{2,1,0:T(2,128)}, u32[]{:S(2)}, u32[]{:S(2)}) collective-permute-start(f32[3,2,2048]{2,1,0:T(2,128)} %get-tuple-element.221), channel_id=1, source_target_pairs={{0,1},{1,2},{2,3},{3,4},{4,5},{5,6},{6,7},{7,8},{8,9},{9,10},{10,1... | collective-permute-start | bytes 147464 | tf_op jit(solution)/shard_map/ppermute | solution.py:16
  52.8 48.9 %collective-permute-start.4 = (f32[3,2,2048]{2,1,0:T(2,128)}, f32[3,2,2048]{2,1,0:T(2,128)}, u32[]{:S(2)}, u32[]{:S(2)}) collective-permute-start(f32[3,2,2048]{2,1,0:T(2,128)} %get-tuple-element.222), channel_id=1, source_target_pairs={{1,0},{2,1},{3,2},{4,3},{5,4},{6,5},{7,6},{8,7},{9,8},{10,9},{11,1... | collective-permute-start | bytes 147464 | tf_op jit(solution)/shard_map/ppermute | solution.py:19
  101.7 26.3 %copy-start.1 = (f32[4,2]{1,0:T(4,128)S(1)}, f32[4,2]{1,0:T(4,128)}, u32[]{:S(2)}) copy-start(f32[4,2]{1,0:T(4,128)} %constant.62.clone) | copy-start | bytes 100
  120.3 6.8 collective-permute-start.5
  122.2 5.1 collective-permute-start.6
  135.6 45.0 %collective-permute-start = (f32[4,2,8,2048]{3,2,1,0:T(8,128)S(1)}, f32[4,2,8,2048]{3,2,1,0:T(8,128)S(1)}, u32[]{:S(2)}, u32[]{:S(2)}) collective-permute-start(f32[4,2,8,2048]{3,2,1,0:T(8,128)S(1)} %pad_maximum_fusion.12), channel_id=1, source_target_pairs={{0,32},{32,64},{64,96},{96,128},{128,160},{160,192},{192,224},{224... | collective-permute-start | bytes 1572872 | tf_op jit(solution)/shard_map/while/body/eval_jaxpr/ppermute | solution.py:27
  188.2 34.4 %collective-permute-start = (f32[4,2,8,2048]{3,2,1,0:T(8,128)S(1)}, f32[4,2,8,2048]{3,2,1,0:T(8,128)S(1)}, u32[]{:S(2)}, u32[]{:S(2)}) collective-permute-start(f32[4,2,8,2048]{3,2,1,0:T(8,128)S(1)} %pad_maximum_fusion.12), channel_id=1, source_target_pairs={{0,32},{32,64},{64,96},{96,128},{128,160},{160,192},{192,224},{224... | collective-permute-start | bytes 1572872 | tf_op jit(solution)/shard_map/while/body/eval_jaxpr/ppermute | solution.py:27
  230.1 92.5 %collective-permute-start = (f32[4,2,8,2048]{3,2,1,0:T(8,128)S(1)}, f32[4,2,8,2048]{3,2,1,0:T(8,128)S(1)}, u32[]{:S(2)}, u32[]{:S(2)}) collective-permute-start(f32[4,2,8,2048]{3,2,1,0:T(8,128)S(1)} %pad_maximum_fusion.12), channel_id=1, source_target_pairs={{0,32},{32,64},{64,96},{96,128},{128,160},{160,192},{192,224},{224... | collective-permute-start | bytes 1572872 | tf_op jit(solution)/shard_map/while/body/eval_jaxpr/ppermute | solution.py:27
  330.2 62.8 %collective-permute-start = (f32[4,2,8,2048]{3,2,1,0:T(8,128)S(1)}, f32[4,2,8,2048]{3,2,1,0:T(8,128)S(1)}, u32[]{:S(2)}, u32[]{:S(2)}) collective-permute-start(f32[4,2,8,2048]{3,2,1,0:T(8,128)S(1)} %pad_maximum_fusion.12), channel_id=1, source_target_pairs={{0,32},{32,64},{64,96},{96,128},{128,160},{160,192},{192,224},{224... | collective-permute-start | bytes 1572872 | tf_op jit(solution)/shard_map/while/body/eval_jaxpr/ppermute | solution.py:27
  400.6 16.1 %collective-permute-start = (f32[4,2,8,2048]{3,2,1,0:T(8,128)S(1)}, f32[4,2,8,2048]{3,2,1,0:T(8,128)S(1)}, u32[]{:S(2)}, u32[]{:S(2)}) collective-permute-start(f32[4,2,8,2048]{3,2,1,0:T(8,128)S(1)} %pad_maximum_fusion.12), channel_id=1, source_target_pairs={{0,32},{32,64},{64,96},{96,128},{128,160},{160,192},{192,224},{224... | collective-permute-start | bytes 1572872 | tf_op jit(solution)/shard_map/while/body/eval_jaxpr/ppermute | solution.py:27
  424.4 89.0 %collective-permute-start = (f32[4,2,8,2048]{3,2,1,0:T(8,128)S(1)}, f32[4,2,8,2048]{3,2,1,0:T(8,128)S(1)}, u32[]{:S(2)}, u32[]{:S(2)}) collective-permute-start(f32[4,2,8,2048]{3,2,1,0:T(8,128)S(1)} %pad_maximum_fusion.12), channel_id=1, source_target_pairs={{0,32},{32,64},{64,96},{96,128},{128,160},{160,192},{192,224},{224... | collective-permute-start | bytes 1572872 | tf_op jit(solution)/shard_map/while/body/eval_jaxpr/ppermute | solution.py:27
  520.9 48.1 %collective-permute-start = (f32[4,2,8,2048]{3,2,1,0:T(8,128)S(1)}, f32[4,2,8,2048]{3,2,1,0:T(8,128)S(1)}, u32[]{:S(2)}, u32[]{:S(2)}) collective-permute-start(f32[4,2,8,2048]{3,2,1,0:T(8,128)S(1)} %pad_maximum_fusion.12), channel_id=1, source_target_pairs={{0,32},{32,64},{64,96},{96,128},{128,160},{160,192},{192,224},{224... | collective-permute-start | bytes 1572872 | tf_op jit(solution)/shard_map/while/body/eval_jaxpr/ppermute | solution.py:27
  576.6 156.1 %collective-permute-start = (f32[4,2,8,2048]{3,2,1,0:T(8,128)S(1)}, f32[4,2,8,2048]{3,2,1,0:T(8,128)S(1)}, u32[]{:S(2)}, u32[]{:S(2)}) collective-permute-start(f32[4,2,8,2048]{3,2,1,0:T(8,128)S(1)} %pad_maximum_fusion.12), channel_id=1, source_target_pairs={{0,32},{32,64},{64,96},{96,128},{128,160},{160,192},{192,224},{224... | collective-permute-start | bytes 1572872 | tf_op jit(solution)/shard_map/while/body/eval_jaxpr/ppermute | solution.py:27
  740.3 91.6 %collective-permute-start = (f32[4,2,8,2048]{3,2,1,0:T(8,128)S(1)}, f32[4,2,8,2048]{3,2,1,0:T(8,128)S(1)}, u32[]{:S(2)}, u32[]{:S(2)}) collective-permute-start(f32[4,2,8,2048]{3,2,1,0:T(8,128)S(1)} %pad_maximum_fusion.12), channel_id=1, source_target_pairs={{0,32},{32,64},{64,96},{96,128},{128,160},{160,192},{192,224},{224... | collective-permute-start | bytes 1572872 | tf_op jit(solution)/shard_map/while/body/eval_jaxpr/ppermute | solution.py:27
  839.5 36.1 %collective-permute-start = (f32[4,2,8,2048]{3,2,1,0:T(8,128)S(1)}, f32[4,2,8,2048]{3,2,1,0:T(8,128)S(1)}, u32[]{:S(2)}, u32[]{:S(2)}) collective-permute-start(f32[4,2,8,2048]{3,2,1,0:T(8,128)S(1)} %pad_maximum_fusion.12), channel_id=1, source_target_pairs={{0,32},{32,64},{64,96},{96,128},{128,160},{160,192},{192,224},{224... | collective-permute-start | bytes 1572872 | tf_op jit(solution)/shard_map/while/body/eval_jaxpr/ppermute | solution.py:27
  883.2 16.0 %collective-permute-start = (f32[4,2,8,2048]{3,2,1,0:T(8,128)S(1)}, f32[4,2,8,2048]{3,2,1,0:T(8,128)S(1)}, u32[]{:S(2)}, u32[]{:S(2)}) collective-permute-start(f32[4,2,8,2048]{3,2,1,0:T(8,128)S(1)} %pad_maximum_fusion.12), channel_id=1, source_target_pairs={{0,32},{32,64},{64,96},{96,128},{128,160},{160,192},{192,224},{224... | collective-permute-start | bytes 1572872 | tf_op jit(solution)/shard_map/while/body/eval_jaxpr/ppermute | solution.py:27
  906.8 24.9 %collective-permute-start = (f32[4,2,8,2048]{3,2,1,0:T(8,128)S(1)}, f32[4,2,8,2048]{3,2,1,0:T(8,128)S(1)}, u32[]{:S(2)}, u32[]{:S(2)}) collective-permute-start(f32[4,2,8,2048]{3,2,1,0:T(8,128)S(1)} %pad_maximum_fusion.12), channel_id=1, source_target_pairs={{0,32},{32,64},{64,96},{96,128},{128,160},{160,192},{192,224},{224... | collective-permute-start | bytes 1572872 | tf_op jit(solution)/shard_map/while/body/eval_jaxpr/ppermute | solution.py:27
  939.2 28.4 %collective-permute-start = (f32[4,2,8,2048]{3,2,1,0:T(8,128)S(1)}, f32[4,2,8,2048]{3,2,1,0:T(8,128)S(1)}, u32[]{:S(2)}, u32[]{:S(2)}) collective-permute-start(f32[4,2,8,2048]{3,2,1,0:T(8,128)S(1)} %pad_maximum_fusion.12), channel_id=1, source_target_pairs={{0,32},{32,64},{64,96},{96,128},{128,160},{160,192},{192,224},{224... | collective-permute-start | bytes 1572872 | tf_op jit(solution)/shard_map/while/body/eval_jaxpr/ppermute | solution.py:27
  975.2 24.6 %collective-permute-start = (f32[4,2,8,2048]{3,2,1,0:T(8,128)S(1)}, f32[4,2,8,2048]{3,2,1,0:T(8,128)S(1)}, u32[]{:S(2)}, u32[]{:S(2)}) collective-permute-start(f32[4,2,8,2048]{3,2,1,0:T(8,128)S(1)} %pad_maximum_fusion.12), channel_id=1, source_target_pairs={{0,32},{32,64},{64,96},{96,128},{128,160},{160,192},{192,224},{224... | collective-permute-start | bytes 1572872 | tf_op jit(solution)/shard_map/while/body/eval_jaxpr/ppermute | solution.py:27
  1007.4 15.9 %collective-permute-start = (f32[4,2,8,2048]{3,2,1,0:T(8,128)S(1)}, f32[4,2,8,2048]{3,2,1,0:T(8,128)S(1)}, u32[]{:S(2)}, u32[]{:S(2)}) collective-permute-start(f32[4,2,8,2048]{3,2,1,0:T(8,128)S(1)} %pad_maximum_fusion.12), channel_id=1, source_target_pairs={{0,32},{32,64},{64,96},{96,128},{128,160},{160,192},{192,224},{224... | collective-permute-start | bytes 1572872 | tf_op jit(solution)/shard_map/while/body/eval_jaxpr/ppermute | solution.py:27
where the time goes:
time: 1030 us
  waiting for transfers between devices  469 us (46%)
  starting transfers between devices  328 us (32%)
  other arithmetic  138 us (13%)
  local copies, waits for them, and re-layouts  43.6 us (4%)
  blocking collectives  36.7 us (4%)
  matrix products  12.7 us (1%)
    ppermute x15, waiting for transfers between devices, from_behind(): return lax.ppermute(value, axis, pairs)  469 us
    ppermute x15, starting transfers between devices, from_behind(): return lax.ppermute(value, axis, pairs)  312 us
    sub x48, other arithmetic, lens_step(): (1.0 - mixing) * previous + mixing * current - bending * bent_rows  105 us
    all_gather x1, blocking collectives, body(): received = lax.all_gather(coarse, 'tile', axis=1, tiled=True)  36.7 us
  transfers between devices with their start and end apart: 21, of which 16 were waited for; matrix products, arithmetic and copies ran while one was open for 2% of the time, Pallas kernels for 0%

commit v1 on v0

--- a/solution.py
+++ b/solution.py
@@ -130,7 +130,8 @@
     short_part = short_rows(convergence_wide, short_kernel)
     row_global = tile_index * coarse_here + 0 + jnp.arange(coarse_here, dtype=jnp.int32)
     coarse = convergence.reshape(plane_count, coarse_here, 4, coarse_cols, 4).mean(axis=(2, 4))
-    received = lax.all_gather(coarse, "tile", axis=1, tiled=True)
+    sent = jnp.stack([coarse] * lax.axis_size("tile"))
+    received = jnp.concatenate(lax.all_to_all(sent, "tile", 0, 0), axis=1)
     span_cols = received.shape[1]
     kernel_block = coarse_kernel(row_global, jnp.arange(span_cols, dtype=jnp.int32), row_scale)
     summed = jnp.einsum("ik,pkx->pix", kernel_block, received, precision=highest)

time: 1030 us -> 991 us (0.962)
  the two profiles are of different devices: /device:TPU:108 before, /device:TPU:106 now
where the time goes in v1:
time: 991 us; the launch traced here: 988 us
  waiting for transfers between devices  613 us (62%)
  starting transfers between devices  187 us (19%)
  other arithmetic  130 us (13%)
  local copies, waits for them, and re-layouts  42.6 us (4%)
  matrix products  12.6 us (1%)
    ppermute x15, waiting for transfers between devices, from_behind(): return lax.ppermute(value, axis, pairs)  611 us
    ppermute x15, starting transfers between devices, from_behind(): return lax.ppermute(value, axis, pairs)  160 us
    sub x48, other arithmetic, lens_step(): (1.0 - mixing) * previous + mixing * current - bending * bent_rows  102 us
  transfers between devices with their start and end apart: 22, of which 19 were waited for; matrix products, arithmetic and copies ran while one was open for 1% of the time, Pallas kernels for 0%

profile of v1, /device:TPU:106, one launch (start us, length us, event | category | flops | bytes accessed | tf_op | source)
XLA Modules:
  0.0 988.4 jit_solution(5103834122238602432)
XLA Ops:
  17.2 6.6 stack.68
  23.8 7.6 fusion.60
  35.4 7.9 reshape.73
  47.4 9.6 all-to-all-start
  73.4 16.4 %fusion.32 = f32[3,8,2048]{2,1,0:T(8,128)S(1)} fusion(f32[3,8,2048]{2,1,0:T(8,128)S(1)} %copy.171, f32[3,8,2048]{2,1,0:T(8,128)S(1)} %bitcast.139, f32[3,2,2048]{2,1,0:T(2,128)S(1)} %collective-permute-done.4, f32[3,2,2048]{2,1,0:T(2,128)S(1)} %collective-permute-done.3, f32[3,12,2052]{2,1,0:T(8,128)S(1)} %select_maximum_fusion.2, f32[]{:T(128)} %bitcast.37, ...), kind=kLoop, calls=%fused_computation.73 | loop fusion | flops 2654208 | bytes 4620388 | tf_op jit(solution)/shard_map/add | solution.py:138
  99.6 881.2 %while.13 = (s32[]{:T(128)}, f32[4,2,8,2048]{3,2,1,0:T(8,128)S(1)}, pred[]{:T(512)}, f32[]{:T(128)}, f32[3]{0:T(128)S(1)}, /*index=5*/f32[]{:T(128)}, f32[3]{0:T...) while((s32[]{:T(128)}, f32[4,2,8,2048]{3,2,1,0:T(8,128)S(1)}, ...), condition=%wide.region_2.3_spmd.clone, body=%wide.region_1.2_spmd.sunk.clone.sunk | while | flops 2818050 | bytes 11469090 | solution.py:167
  106.9 9.1 collective-permute-start
  116.0 47.5 %collective-permute-done = f32[4,2,8,2048]{3,2,1,0:T(8,128)S(1)} collective-permute-done((f32[4,2,8,2048]{3,2,1,0:T(8,128)S(1)}, f32[4,2,8,2048]{3,2,1,0:T(8,128)S(1)}, u32[]{:S(2)}, u32[]{:S(2)}) %collective-permute-start) | collective-permute-done | bytes 524320 | tf_op jit(solution)/shard_map/while/body/eval_jaxpr/ppermute | solution.py:27
  170.9 6.4 collective-permute-start
  177.3 36.3 %collective-permute-done = f32[4,2,8,2048]{3,2,1,0:T(8,128)S(1)} collective-permute-done((f32[4,2,8,2048]{3,2,1,0:T(8,128)S(1)}, f32[4,2,8,2048]{3,2,1,0:T(8,128)S(1)}, u32[]{:S(2)}, u32[]{:S(2)}) %collective-permute-start) | collective-permute-done | bytes 524320 | tf_op jit(solution)/shard_map/while/body/eval_jaxpr/ppermute | solution.py:27
  223.3 67.9 %collective-permute-done = f32[4,2,8,2048]{3,2,1,0:T(8,128)S(1)} collective-permute-done((f32[4,2,8,2048]{3,2,1,0:T(8,128)S(1)}, f32[4,2,8,2048]{3,2,1,0:T(8,128)S(1)}, u32[]{:S(2)}, u32[]{:S(2)}) %collective-permute-start) | collective-permute-done | bytes 524320 | tf_op jit(solution)/shard_map/while/body/eval_jaxpr/ppermute | solution.py:27
  298.5 8.3 collective-permute-start
  306.8 89.2 %collective-permute-done = f32[4,2,8,2048]{3,2,1,0:T(8,128)S(1)} collective-permute-done((f32[4,2,8,2048]{3,2,1,0:T(8,128)S(1)}, f32[4,2,8,2048]{3,2,1,0:T(8,128)S(1)}, u32[]{:S(2)}, u32[]{:S(2)}) %collective-permute-start) | collective-permute-done | bytes 524320 | tf_op jit(solution)/shard_map/while/body/eval_jaxpr/ppermute | solution.py:27
  405.3 40.3 %collective-permute-done = f32[4,2,8,2048]{3,2,1,0:T(8,128)S(1)} collective-permute-done((f32[4,2,8,2048]{3,2,1,0:T(8,128)S(1)}, f32[4,2,8,2048]{3,2,1,0:T(8,128)S(1)}, u32[]{:S(2)}, u32[]{:S(2)}) %collective-permute-start) | collective-permute-done | bytes 524320 | tf_op jit(solution)/shard_map/while/body/eval_jaxpr/ppermute | solution.py:27
  452.9 8.3 collective-permute-start
  461.2 56.1 %collective-permute-done = f32[4,2,8,2048]{3,2,1,0:T(8,128)S(1)} collective-permute-done((f32[4,2,8,2048]{3,2,1,0:T(8,128)S(1)}, f32[4,2,8,2048]{3,2,1,0:T(8,128)S(1)}, u32[]{:S(2)}, u32[]{:S(2)}) %collective-permute-start) | collective-permute-done | bytes 524320 | tf_op jit(solution)/shard_map/while/body/eval_jaxpr/ppermute | solution.py:27
  526.6 46.7 %collective-permute-done = f32[4,2,8,2048]{3,2,1,0:T(8,128)S(1)} collective-permute-done((f32[4,2,8,2048]{3,2,1,0:T(8,128)S(1)}, f32[4,2,8,2048]{3,2,1,0:T(8,128)S(1)}, u32[]{:S(2)}, u32[]{:S(2)}) %collective-permute-start) | collective-permute-done | bytes 524320 | tf_op jit(solution)/shard_map/while/body/eval_jaxpr/ppermute | solution.py:27
  580.7 6.9 collective-permute-start
  587.6 30.3 %collective-permute-done = f32[4,2,8,2048]{3,2,1,0:T(8,128)S(1)} collective-permute-done((f32[4,2,8,2048]{3,2,1,0:T(8,128)S(1)}, f32[4,2,8,2048]{3,2,1,0:T(8,128)S(1)}, u32[]{:S(2)}, u32[]{:S(2)}) %collective-permute-start) | collective-permute-done | bytes 524320 | tf_op jit(solution)/shard_map/while/body/eval_jaxpr/ppermute | solution.py:27
  625.3 65.3 %collective-permute-start = (f32[4,2,8,2048]{3,2,1,0:T(8,128)S(1)}, f32[4,2,8,2048]{3,2,1,0:T(8,128)S(1)}, u32[]{:S(2)}, u32[]{:S(2)}) collective-permute-start(f32[4,2,8,2048]{3,2,1,0:T(8,128)S(1)} %pad_maximum_fusion.12), channel_id=1, source_target_pairs={{0,32},{32,64},{64,96},{96,128},{128,160},{160,192},{192,224},{224... | collective-permute-start | bytes 1572872 | tf_op jit(solution)/shard_map/while/body/eval_jaxpr/ppermute | solution.py:27
  690.6 20.3 %collective-permute-done = f32[4,2,8,2048]{3,2,1,0:T(8,128)S(1)} collective-permute-done((f32[4,2,8,2048]{3,2,1,0:T(8,128)S(1)}, f32[4,2,8,2048]{3,2,1,0:T(8,128)S(1)}, u32[]{:S(2)}, u32[]{:S(2)}) %collective-permute-start) | collective-permute-done | bytes 524320 | tf_op jit(solution)/shard_map/while/body/eval_jaxpr/ppermute | solution.py:27
  718.2 21.8 %collective-permute-start = (f32[4,2,8,2048]{3,2,1,0:T(8,128)S(1)}, f32[4,2,8,2048]{3,2,1,0:T(8,128)S(1)}, u32[]{:S(2)}, u32[]{:S(2)}) collective-permute-start(f32[4,2,8,2048]{3,2,1,0:T(8,128)S(1)} %pad_maximum_fusion.12), channel_id=1, source_target_pairs={{0,32},{32,64},{64,96},{96,128},{128,160},{160,192},{192,224},{224... | collective-permute-start | bytes 1572872 | tf_op jit(solution)/shard_map/while/body/eval_jaxpr/ppermute | solution.py:27
  740.1 85.0 %collective-permute-done = f32[4,2,8,2048]{3,2,1,0:T(8,128)S(1)} collective-permute-done((f32[4,2,8,2048]{3,2,1,0:T(8,128)S(1)}, f32[4,2,8,2048]{3,2,1,0:T(8,128)S(1)}, u32[]{:S(2)}, u32[]{:S(2)}) %collective-permute-start) | collective-permute-done | bytes 524320 | tf_op jit(solution)/shard_map/while/body/eval_jaxpr/ppermute | solution.py:27
  834.3 29.3 %collective-permute-done = f32[4,2,8,2048]{3,2,1,0:T(8,128)S(1)} collective-permute-done((f32[4,2,8,2048]{3,2,1,0:T(8,128)S(1)}, f32[4,2,8,2048]{3,2,1,0:T(8,128)S(1)}, u32[]{:S(2)}, u32[]{:S(2)}) %collective-permute-start) | collective-permute-done | bytes 524320 | tf_op jit(solution)/shard_map/while/body/eval_jaxpr/ppermute | solution.py:27
  871.0 8.3 collective-permute-start
  879.3 23.4 %collective-permute-done = f32[4,2,8,2048]{3,2,1,0:T(8,128)S(1)} collective-permute-done((f32[4,2,8,2048]{3,2,1,0:T(8,128)S(1)}, f32[4,2,8,2048]{3,2,1,0:T(8,128)S(1)}, u32[]{:S(2)}, u32[]{:S(2)}) %collective-permute-start) | collective-permute-done | bytes 524320 | tf_op jit(solution)/shard_map/while/body/eval_jaxpr/ppermute | solution.py:27
  910.0 5.9 collective-permute-start
  915.9 13.7 %collective-permute-done = f32[4,2,8,2048]{3,2,1,0:T(8,128)S(1)} collective-permute-done((f32[4,2,8,2048]{3,2,1,0:T(8,128)S(1)}, f32[4,2,8,2048]{3,2,1,0:T(8,128)S(1)}, u32[]{:S(2)}, u32[]{:S(2)}) %collective-permute-start) | collective-permute-done | bytes 524320 | tf_op jit(solution)/shard_map/while/body/eval_jaxpr/ppermute | solution.py:27
  936.9 5.8 collective-permute-start
  942.7 12.9 %collective-permute-done = f32[4,2,8,2048]{3,2,1,0:T(8,128)S(1)} collective-permute-done((f32[4,2,8,2048]{3,2,1,0:T(8,128)S(1)}, f32[4,2,8,2048]{3,2,1,0:T(8,128)S(1)}, u32[]{:S(2)}, u32[]{:S(2)}) %collective-permute-start) | collective-permute-done | bytes 524320 | tf_op jit(solution)/shard_map/while/body/eval_jaxpr/ppermute | solution.py:27
  963.0 5.8 collective-permute-start
  968.8 11.9 %collective-permute-done = f32[4,2,8,2048]{3,2,1,0:T(8,128)S(1)} collective-permute-done((f32[4,2,8,2048]{3,2,1,0:T(8,128)S(1)}, f32[4,2,8,2048]{3,2,1,0:T(8,128)S(1)}, u32[]{:S(2)}, u32[]{:S(2)}) %collective-permute-start) | collective-permute-done | bytes 524320 | tf_op jit(solution)/shard_map/while/body/eval_jaxpr/ppermute | solution.py:27
  (235 shorter events, 174.4 us)
Async XLA Ops:
  0.0 23.8 %copy-start = (f32[32,9]{0,1:T(8,128)S(1)}, f32[32,9]{0,1:T(8,128)}, u32[]{:S(2)}) copy-start(f32[32,9]{0,1:T(8,128)} %param.11) | copy-start | bytes 3460
  1.1 7.4 collective-permute-start.1
  3.0 5.5 collective-permute-start.2
  23.8 7.6 copy-start.4
  23.8 7.6 copy-start.5
  35.4 21.7 %copy-start.3 = (s32[48]{0:T(128)S(1)}, s32[48]{0:T(128)}, u32[]{:S(2)}) copy-start(s32[48]{0:T(128)} %param.10) | copy-start | bytes 580
  35.4 22.5 %copy-start.2 = (f32[5,5]{1,0:T(8,128)S(1)}, f32[5,5]{1,0:T(8,128)}, u32[]{:S(2)}) copy-start(f32[5,5]{1,0:T(8,128)} %param.14) | copy-start | bytes 304
  47.4 19.7 %all-to-all-start = ((f32[32,3,2,512]{3,2,1,0:T(2,128)}), f32[32,3,2,512]{3,2,1,0:T(2,128)S(1)}, u32[]{:S(2)}, u32[]{:S(2)}) async-start(f32[32,3,2,512]{3,2,1,0:T(2,128)} %stack.69), calls=%async_computation | async-start | bytes 786432 | tf_op jit(solution)/shard_map/all_to_all | solution.py:134
  59.3 5.8 collective-permute-start.3
  61.4 5.2 collective-permute-start.4
  71.1 28.5 %copy-start.1 = (f32[4,2]{1,0:T(4,128)S(1)}, f32[4,2]{1,0:T(4,128)}, u32[]{:S(2)}) copy-start(f32[4,2]{1,0:T(4,128)} %constant.62.clone) | copy-start | bytes 100
  89.8 8.4 collective-permute-start.5
  93.7 5.1 collective-permute-start.6
  106.9 56.6 %collective-permute-start = (f32[4,2,8,2048]{3,2,1,0:T(8,128)S(1)}, f32[4,2,8,2048]{3,2,1,0:T(8,128)S(1)}, u32[]{:S(2)}, u32[]{:S(2)}) collective-permute-start(f32[4,2,8,2048]{3,2,1,0:T(8,128)S(1)} %pad_maximum_fusion.12), channel_id=1, source_target_pairs={{0,32},{32,64},{64,96},{96,128},{128,160},{160,192},{192,224},{224... | collective-permute-start | bytes 1572872 | tf_op jit(solution)/shard_map/while/body/eval_jaxpr/ppermute | solution.py:27
  170.9 42.8 %collective-permute-start = (f32[4,2,8,2048]{3,2,1,0:T(8,128)S(1)}, f32[4,2,8,2048]{3,2,1,0:T(8,128)S(1)}, u32[]{:S(2)}, u32[]{:S(2)}) collective-permute-start(f32[4,2,8,2048]{3,2,1,0:T(8,128)S(1)} %pad_maximum_fusion.12), channel_id=1, source_target_pairs={{0,32},{32,64},{64,96},{96,128},{128,160},{160,192},{192,224},{224... | collective-permute-start | bytes 1572872 | tf_op jit(solution)/shard_map/while/body/eval_jaxpr/ppermute | solution.py:27
  221.0 70.2 %collective-permute-start = (f32[4,2,8,2048]{3,2,1,0:T(8,128)S(1)}, f32[4,2,8,2048]{3,2,1,0:T(8,128)S(1)}, u32[]{:S(2)}, u32[]{:S(2)}) collective-permute-start(f32[4,2,8,2048]{3,2,1,0:T(8,128)S(1)} %pad_maximum_fusion.12), channel_id=1, source_target_pairs={{0,32},{32,64},{64,96},{96,128},{128,160},{160,192},{192,224},{224... | collective-permute-start | bytes 1572872 | tf_op jit(solution)/shard_map/while/body/eval_jaxpr/ppermute | solution.py:27
  298.5 97.5 %collective-permute-start = (f32[4,2,8,2048]{3,2,1,0:T(8,128)S(1)}, f32[4,2,8,2048]{3,2,1,0:T(8,128)S(1)}, u32[]{:S(2)}, u32[]{:S(2)}) collective-permute-start(f32[4,2,8,2048]{3,2,1,0:T(8,128)S(1)} %pad_maximum_fusion.12), channel_id=1, source_target_pairs={{0,32},{32,64},{64,96},{96,128},{128,160},{160,192},{192,224},{224... | collective-permute-start | bytes 1572872 | tf_op jit(solution)/shard_map/while/body/eval_jaxpr/ppermute | solution.py:27
  403.4 42.2 %collective-permute-start = (f32[4,2,8,2048]{3,2,1,0:T(8,128)S(1)}, f32[4,2,8,2048]{3,2,1,0:T(8,128)S(1)}, u32[]{:S(2)}, u32[]{:S(2)}) collective-permute-start(f32[4,2,8,2048]{3,2,1,0:T(8,128)S(1)} %pad_maximum_fusion.12), channel_id=1, source_target_pairs={{0,32},{32,64},{64,96},{96,128},{128,160},{160,192},{192,224},{224... | collective-permute-start | bytes 1572872 | tf_op jit(solution)/shard_map/while/body/eval_jaxpr/ppermute | solution.py:27
  452.9 64.4 %collective-permute-start = (f32[4,2,8,2048]{3,2,1,0:T(8,128)S(1)}, f32[4,2,8,2048]{3,2,1,0:T(8,128)S(1)}, u32[]{:S(2)}, u32[]{:S(2)}) collective-permute-start(f32[4,2,8,2048]{3,2,1,0:T(8,128)S(1)} %pad_maximum_fusion.12), channel_id=1, source_target_pairs={{0,32},{32,64},{64,96},{96,128},{128,160},{160,192},{192,224},{224... | collective-permute-start | bytes 1572872 | tf_op jit(solution)/shard_map/while/body/eval_jaxpr/ppermute | solution.py:27
  524.7 48.6 %collective-permute-start = (f32[4,2,8,2048]{3,2,1,0:T(8,128)S(1)}, f32[4,2,8,2048]{3,2,1,0:T(8,128)S(1)}, u32[]{:S(2)}, u32[]{:S(2)}) collective-permute-start(f32[4,2,8,2048]{3,2,1,0:T(8,128)S(1)} %pad_maximum_fusion.12), channel_id=1, source_target_pairs={{0,32},{32,64},{64,96},{96,128},{128,160},{160,192},{192,224},{224... | collective-permute-start | bytes 1572872 | tf_op jit(solution)/shard_map/while/body/eval_jaxpr/ppermute | solution.py:27
  580.7 37.2 %collective-permute-start = (f32[4,2,8,2048]{3,2,1,0:T(8,128)S(1)}, f32[4,2,8,2048]{3,2,1,0:T(8,128)S(1)}, u32[]{:S(2)}, u32[]{:S(2)}) collective-permute-start(f32[4,2,8,2048]{3,2,1,0:T(8,128)S(1)} %pad_maximum_fusion.12), channel_id=1, source_target_pairs={{0,32},{32,64},{64,96},{96,128},{128,160},{160,192},{192,224},{224... | collective-permute-start | bytes 1572872 | tf_op jit(solution)/shard_map/while/body/eval_jaxpr/ppermute | solution.py:27
  625.3 85.6 %collective-permute-start = (f32[4,2,8,2048]{3,2,1,0:T(8,128)S(1)}, f32[4,2,8,2048]{3,2,1,0:T(8,128)S(1)}, u32[]{:S(2)}, u32[]{:S(2)}) collective-permute-start(f32[4,2,8,2048]{3,2,1,0:T(8,128)S(1)} %pad_maximum_fusion.12), channel_id=1, source_target_pairs={{0,32},{32,64},{64,96},{96,128},{128,160},{160,192},{192,224},{224... | collective-permute-start | bytes 1572872 | tf_op jit(solution)/shard_map/while/body/eval_jaxpr/ppermute | solution.py:27
  718.2 106.8 %collective-permute-start = (f32[4,2,8,2048]{3,2,1,0:T(8,128)S(1)}, f32[4,2,8,2048]{3,2,1,0:T(8,128)S(1)}, u32[]{:S(2)}, u32[]{:S(2)}) collective-permute-start(f32[4,2,8,2048]{3,2,1,0:T(8,128)S(1)} %pad_maximum_fusion.12), channel_id=1, source_target_pairs={{0,32},{32,64},{64,96},{96,128},{128,160},{160,192},{192,224},{224... | collective-permute-start | bytes 1572872 | tf_op jit(solution)/shard_map/while/body/eval_jaxpr/ppermute | solution.py:27
  832.4 31.3 %collective-permute-start = (f32[4,2,8,2048]{3,2,1,0:T(8,128)S(1)}, f32[4,2,8,2048]{3,2,1,0:T(8,128)S(1)}, u32[]{:S(2)}, u32[]{:S(2)}) collective-permute-start(f32[4,2,8,2048]{3,2,1,0:T(8,128)S(1)} %pad_maximum_fusion.12), channel_id=1, source_target_pairs={{0,32},{32,64},{64,96},{96,128},{128,160},{160,192},{192,224},{224... | collective-permute-start | bytes 1572872 | tf_op jit(solution)/shard_map/while/body/eval_jaxpr/ppermute | solution.py:27
  871.0 31.6 %collective-permute-start = (f32[4,2,8,2048]{3,2,1,0:T(8,128)S(1)}, f32[4,2,8,2048]{3,2,1,0:T(8,128)S(1)}, u32[]{:S(2)}, u32[]{:S(2)}) collective-permute-start(f32[4,2,8,2048]{3,2,1,0:T(8,128)S(1)} %pad_maximum_fusion.12), channel_id=1, source_target_pairs={{0,32},{32,64},{64,96},{96,128},{128,160},{160,192},{192,224},{224... | collective-permute-start | bytes 1572872 | tf_op jit(solution)/shard_map/while/body/eval_jaxpr/ppermute | solution.py:27
  910.0 19.6 %collective-permute-start = (f32[4,2,8,2048]{3,2,1,0:T(8,128)S(1)}, f32[4,2,8,2048]{3,2,1,0:T(8,128)S(1)}, u32[]{:S(2)}, u32[]{:S(2)}) collective-permute-start(f32[4,2,8,2048]{3,2,1,0:T(8,128)S(1)} %pad_maximum_fusion.12), channel_id=1, source_target_pairs={{0,32},{32,64},{64,96},{96,128},{128,160},{160,192},{192,224},{224... | collective-permute-start | bytes 1572872 | tf_op jit(solution)/shard_map/while/body/eval_jaxpr/ppermute | solution.py:27
  936.9 18.7 %collective-permute-start = (f32[4,2,8,2048]{3,2,1,0:T(8,128)S(1)}, f32[4,2,8,2048]{3,2,1,0:T(8,128)S(1)}, u32[]{:S(2)}, u32[]{:S(2)}) collective-permute-start(f32[4,2,8,2048]{3,2,1,0:T(8,128)S(1)} %pad_maximum_fusion.12), channel_id=1, source_target_pairs={{0,32},{32,64},{64,96},{96,128},{128,160},{160,192},{192,224},{224... | collective-permute-start | bytes 1572872 | tf_op jit(solution)/shard_map/while/body/eval_jaxpr/ppermute | solution.py:27
  963.0 17.7 %collective-permute-start = (f32[4,2,8,2048]{3,2,1,0:T(8,128)S(1)}, f32[4,2,8,2048]{3,2,1,0:T(8,128)S(1)}, u32[]{:S(2)}, u32[]{:S(2)}) collective-permute-start(f32[4,2,8,2048]{3,2,1,0:T(8,128)S(1)} %pad_maximum_fusion.12), channel_id=1, source_target_pairs={{0,32},{32,64},{64,96},{96,128},{128,160},{160,192},{192,224},{224... | collective-permute-start | bytes 1572872 | tf_op jit(solution)/shard_map/while/body/eval_jaxpr/ppermute | solution.py:27
